TPU v7x, 256 devices: a whole 4x4x8 slice. The times are simulated.
256 devices in a mesh: req: 32 (over y, x, z_hi), tp: 8 (over z_lo, core).
Axes of the slice: x: 4, y: 4, z: 8 (z_hi: 2, z_lo: 4; z = z_hi * 4 + z_lo), core: 2. Of those that a mesh axis runs over, the one named last changes fastest.
Arguments:
- residual: bfloat16 [8192, 2304], P('req'), may hold values from -58 to 58
- context: bfloat16 [8192, 2304], P('req', 'tp'), may hold values from -6 to 6
- attention_output_weight: bfloat16 [2304, 2304], P('tp'), may hold values from -0.1875 to 0.1875
- adapter_down_maps: bfloat16 [64, 2304, 16], P('req', 'tp'), may hold values from -0.125 to 0.125
- adapter_up_maps: bfloat16 [64, 16, 2304], P('req'), may hold values from -1.5 to 1.5
- adapter_storage_row: int32 [64], replicated, may hold values from 0 to 63, each once
- active_adapters: int32 [16], replicated, may hold values from 0 to 63, as said below
- request_token_length: int32 [32, 4], P('req'), may hold values from 1 to 128, 256 in all within a row
- request_adapter_entry: int32 [32, 4], P('req'), may hold values from 0 to 15
- expert_norm_gain: bfloat16 [2304], replicated, may hold values from 0.099609375 to 1.8984375
- router_projection: bfloat16 [2304, 8], replicated, may hold values from -0.125 to 0.125
- expert_choice_pairs: int32 [8192, 2], P('req'), may hold values from 0 to 7, all different within a row; in each aligned block of 256 rows (0 to 255, 256 to 511, ...) at most 80 rows name the same one
- expert_gate_weight: bfloat16 [32, 2304, 5760], P('req', None, 'tp'), as said below
- expert_up_weight: bfloat16 [32, 2304, 5760], P('req', None, 'tp'), as said below
- expert_down_weight: bfloat16 [32, 5760, 2304], P('req', 'tp'), as said below
Outputs:
- layer_out: bfloat16 [8192, 2304], P('req', 'tp')
Inputs may be any that keep to these rules, and one draw needn't show every extreme that they name: `active_adapters`: 16 different adapter numbers, 0 and 63 among them. `adapter_storage_row`: every stored row appears once. `request_token_length`: each group's lengths sum to 256; the longest request of a group has exactly half of 256 tokens. `expert_choice_pairs`: each row names two different experts; within the 256 rows of one group no expert is named by more than 80 rows, a bound that some block reaches. `expert_gate_weight`: the 4 holders c * 8 + e of expert e hold the same weights. `expert_up_weight`: the 4 holders c * 8 + e of expert e hold the same weights. `expert_down_weight`: the 4 holders c * 8 + e of expert e hold the same weights.
All inputs are finite; a program needn't handle non-finite values.
Results may differ from a plain program's by a relative error of at most 0.0095.
Values may be sent and summed in bfloat16 or wider, within the bound.
A program may use at most 128 MiB of HBM per device.

v0:
```python
import jax
import jax.numpy as jnp
from jax import lax
from jax.sharding import Mesh
from jax.sharding import PartitionSpec as P

CAP = 80
NORM_EPS = 1e-05
REQ = ("ry", "rxz")


def segment_onehot(request_token_length, token_count):
    bounds = jnp.cumsum(request_token_length[0])
    position = jnp.arange(token_count, dtype=jnp.int32)
    segment = jnp.sum((position[:, None] >= bounds[None, :]).astype(jnp.int32), axis=1)
    slot_range = jnp.arange(request_token_length.shape[1], dtype=jnp.int32)
    return segment[:, None] == slot_range[None, :]


def route_tables(expert_choice_pairs, expert_count, capacity):
    expert_ids = jnp.arange(expert_count, dtype=jnp.int32)
    first_hit = expert_choice_pairs[None, :, 0] == expert_ids[:, None]
    second_hit = expert_choice_pairs[None, :, 1] == expert_ids[:, None]
    chosen = first_hit | second_hit
    slot_of = jnp.cumsum(chosen.astype(jnp.int32), axis=1) - 1
    slot_range = jnp.arange(capacity, dtype=jnp.int32)
    placement = chosen[:, None, :] & (slot_of[:, None, :] == slot_range[None, :, None])
    return (placement, first_hit, second_hit)


def on_device(
    residual,
    context,
    attention_output_weight,
    adapter_down_maps,
    adapter_up_maps,
    adapter_storage_row,
    active_adapters,
    request_token_length,
    request_adapter_entry,
    expert_norm_gain,
    router_projection,
    expert_choice_pairs,
    expert_gate_weight,
    expert_up_weight,
    expert_down_weight,
):
    token_count = residual.shape[0]
    hidden_width = residual.shape[1]
    feature_share = context.shape[1]
    local_rows = adapter_down_maps.shape[0]
    adapter_rank_size = adapter_down_maps.shape[2]
    request_count = request_token_length.shape[1]
    share_width = hidden_width // lax.axis_size("tp")
    share_start = lax.axis_index("tp") * share_width
    up_slice = lax.dynamic_slice_in_dim(adapter_up_maps, share_start, share_width, 2)
    packed = jnp.concatenate(
        [
            adapter_down_maps.reshape(local_rows, feature_share * adapter_rank_size),
            up_slice.reshape(local_rows, adapter_rank_size * share_width),
        ],
        axis=1,
    )
    all_packed = lax.all_gather(packed, REQ, axis=0, tiled=True)
    request_rows = adapter_storage_row[active_adapters[request_adapter_entry[0]]]
    picked = all_packed[request_rows]
    down_req = picked[:, : feature_share * adapter_rank_size].reshape(
        request_count, feature_share, adapter_rank_size
    )
    up_req = picked[:, feature_share * adapter_rank_size :].reshape(
        request_count * adapter_rank_size, share_width
    )
    down_joined = jnp.transpose(down_req, (1, 0, 2)).reshape(
        feature_share, request_count * adapter_rank_size
    )
    segment_hot = segment_onehot(request_token_length, token_count)
    low_all = jnp.dot(context, down_joined, preferred_element_type=jnp.float32)
    reduced_mask = jnp.repeat(segment_hot, adapter_rank_size, axis=1)
    low_part = jnp.where(reduced_mask, low_all, 0.0)
    low_total = lax.psum(low_part, "tp").astype(jnp.bfloat16)
    lora_share = jnp.dot(low_total, up_req, preferred_element_type=jnp.float32)
    base = jnp.dot(context, attention_output_weight, preferred_element_type=jnp.float32)
    base_share = lax.dynamic_slice_in_dim(base, share_start, share_width, 1)
    head_part = lax.dynamic_update_slice_in_dim(base, base_share + lora_share, share_start, 1)
    gain_all = expert_norm_gain.astype(jnp.float32)
    head_sum = lax.psum(head_part.astype(jnp.bfloat16), "tp").astype(jnp.float32)
    blended_rows = residual.astype(jnp.float32) + head_sum
    mean_square = jnp.mean(blended_rows * blended_rows, axis=1, keepdims=True)
    normed = (blended_rows * lax.rsqrt(mean_square + NORM_EPS) * gain_all).astype(jnp.bfloat16)
    mixed_share = lax.dynamic_slice_in_dim(blended_rows, share_start, share_width, 1)
    logits = jnp.dot(normed, router_projection, preferred_element_type=jnp.float32)
    expert_count = router_projection.shape[1]
    expert_range = jnp.arange(expert_count, dtype=jnp.int32)
    logit_first = jnp.sum(
        jnp.where(expert_choice_pairs[:, 0:1] == expert_range[None, :], logits, 0.0), axis=1
    )
    logit_second = jnp.sum(
        jnp.where(expert_choice_pairs[:, 1:2] == expert_range[None, :], logits, 0.0), axis=1
    )
    weight_first = 1.0 / (1.0 + jnp.exp(logit_second - logit_first))
    weight_second = 1.0 / (1.0 + jnp.exp(logit_first - logit_second))
    placement, first_hit, second_hit = route_tables(expert_choice_pairs, expert_count, CAP)
    send_rows = jnp.einsum(
        "est,td->esd", placement.astype(jnp.bfloat16), normed, preferred_element_type=jnp.float32
    ).astype(jnp.bfloat16)
    rows_in = lax.all_to_all(send_rows, "rxz", split_axis=0, concat_axis=0, tiled=True)
    rows_flat = rows_in.reshape(expert_count * CAP, hidden_width)
    gate_value = jnp.dot(rows_flat, expert_gate_weight[0], preferred_element_type=jnp.float32)
    up_value = jnp.dot(rows_flat, expert_up_weight[0], preferred_element_type=jnp.float32)
    hidden = (jax.nn.silu(gate_value) * up_value).astype(jnp.bfloat16)
    partial_value = jnp.dot(hidden, expert_down_weight[0], preferred_element_type=jnp.float32)
    returned = lax.all_to_all(
        partial_value.astype(jnp.bfloat16).reshape(expert_count, CAP, hidden_width),
        "rxz",
        split_axis=0,
        concat_axis=0,
        tiled=True,
    )
    token_weight = jnp.where(first_hit, weight_first[None, :], 0.0) + jnp.where(
        second_hit, weight_second[None, :], 0.0
    )
    scaled_place = placement.astype(jnp.float32) * token_weight[:, None, :]
    contribution = jnp.einsum(
        "est,esd->td",
        scaled_place,
        returned.astype(jnp.float32),
        precision=lax.Precision.HIGHEST,
        preferred_element_type=jnp.float32,
    )
    moe_share = lax.psum_scatter(
        contribution.astype(jnp.bfloat16), "tp", scatter_dimension=1, tiled=True
    ).astype(jnp.float32)
    return (mixed_share + moe_share).astype(jnp.bfloat16)


def solution(mesh):
    req_size = mesh.shape["req"]
    plane = 8
    split_mesh = Mesh(
        mesh.devices.reshape(req_size // plane, plane, mesh.shape["tp"]), ("ry", "rxz", "tp")
    )
    return jax.shard_map(
        on_device,
        mesh=split_mesh,
        in_specs=(
            P(REQ, None),
            P(REQ, "tp"),
            P("tp", None),
            P(REQ, "tp", None),
            P(REQ, None, None),
            P(),
            P(),
            P(REQ, None),
            P(REQ, None),
            P(),
            P(),
            P(REQ, None),
            P(REQ, None, "tp"),
            P(REQ, None, "tp"),
            P(REQ, "tp", None),
        ),
        out_specs=P(REQ, "tp"),
        check_vma=False,
    )
```

profile of v0, /device:TPU:4, one launch (start us, length us, event | category | flops | bytes accessed | tf_op | source)
XLA Modules:
  0.0 434.4 jit_solution(16234100951384589022)
XLA Ops:
  6.5 0.0 copy-start
  6.5 0.0 all-gather.3.cloned.1.call-start
  6.5 1.0 constant_dynamic-slice_fusion
  7.5 0.1 reshape.268
  7.6 0.9 copy.29
  8.5 0.2 reshape.267
  8.7 0.7 maximum_bitcast_fusion
  9.3 0.0 all-gather.3.cloned.1.call-update
  9.4 0.0 all-reduce.2.cloned.1.call-start
  9.4 0.8 reduce-window.18
  10.2 0.7 fusion.27
  10.9 1.3 gather_fusion
  12.2 1.3 gather_fusion.1
  13.5 0.1 convert_reduce_fusion
  13.6 3.6 fusion.35
  17.2 0.0 copy-start.4
  17.2 77.7 %all-gather.3.cloned.1.call-done = bf16[32,2,9216]{2,1,0:T(2,128)(2,1)} async-done(((bf16[1,2,9216]{2,1,0:T(2,128)(2,1)}), bf16[32,2,9216]{2,1,0:T(2,128)(2,1)}) %all-gather.3.cloned.1.call-update) | async-done | bytes 1179664 | tf_op jit(solution)/shard_map/all_gather | solution.py:64
  94.9 2.3 reshape.300
  97.3 2.1 gather_fusion.2
  99.4 0.6 fusion.33
  100.0 1.5 reshape.271
  101.5 1.7 reshape.269
  103.3 1.7 copy.30
  105.0 0.0 copy-done.4
  105.0 1.0 fusion.10
  106.0 26.3 %psum.14 = bf16[256,64]{0,1:T(8,128)(2,1)S(1)} all-reduce(f32[256,64]{0,1:T(8,128)S(1)} %fusion.10), channel_id=1, replica_groups=mesh['ry'=4,'rxz'=8,'tp'=8] {'tp'}, use_global_device_ids=true, to_apply=%region_2.3 | all-reduce | flops 16384 | bytes 98304 | tf_op jit(solution)/shard_map/psum | solution.py:80
  132.3 2.1 convolution_add_fusion
  134.4 3.5 dynamic_update_slice.3
  137.9 0.0 copy-start.6
  137.9 0.0 copy-start.5
  137.9 2.8 convert_element_type.49
  140.7 0.0 all-reduce.2.cloned.1.call-update
  140.7 0.0 copy-done.6
  140.8 0.6 reduce-window.19
  141.3 0.2 slice_reduce_fusion
  141.6 0.0 copy-done.5
  141.6 0.1 add_bitcast_fusion
  141.7 69.1 %all-reduce.2.cloned.1.call-done = bf16[256,2304]{1,0:T(8,128)(2,1)} async-done(((bf16[256,2304]{1,0:T(8,128)(2,1)}), bf16[256,2304]{1,0:T(8,128)(2,1)}) %all-reduce.2.cloned.1.call-update) | async-done | bytes 1179664 | tf_op jit(solution)/shard_map/psum | solution.py:86
  210.8 0.0 copy-start.1
  210.8 0.0 copy-start.2
  210.8 3.6 convert_add_fusion
  214.4 0.0 copy-done.1
  214.4 0.0 copy-done.2
  214.4 1.2 convolution_convert_fusion.1
  215.6 0.0 copy-start.7
  215.6 74.4 %all_to_all.10 = bf16[8,80,2304]{2,1,0:T(8,128)(2,1)S(1)} all-to-all(bf16[8,80,2304]{2,1,0:T(8,128)(2,1)S(1)} %convolution_convert_fusion.1), channel_id=1, replica_groups=mesh['ry'=4,'rxz'=8,'tp'=8] {'rxz'}, dimensions={0} | all-to-all | bytes 5898240 | tf_op jit(solution)/shard_map/all_to_all | solution.py:106
  290.0 0.0 copy-start.3
  290.0 1.6 copy-done.3
  291.7 0.0 copy-done.7
  291.7 4.0 fusion.5
  295.6 0.0 copy-done
  295.6 14.5 %convolution_convert_fusion = bf16[640,2304]{1,0:T(8,128)(2,1)} fusion(bf16[1,720,2304]{2,1,0:T(8,128)(2,1)S(1)} %copy-done, f32[640,720]{0,1:T(8,128)} %fusion.5, bf16[640,2304]{1,0:T(8,128)(2,1)} %bitcast.68, bf16[1,2304,720]{1,2,0:T(8,128)(2,1)} %param.28), kind=kOutput, calls=%fused_computation.3 | convolution fusion | flops 4250972160 | bytes 14376960 | tf_op jit(solution)/shard_map/dot_general | solution.py:111
  310.1 0.0 copy-start.8
  310.2 7.4 %all-to-all-start.1 = ((bf16[8,80,2304]{2,1,0:T(8,128)(2,1)}), bf16[8,80,2304]{2,1,0:T(8,128)(2,1)}, u32[]{:S(2)}, u32[]{:S(2)}) async-start(bf16[8,80,2304]{2,1,0:T(8,128)(2,1)} %bitcast.66), calls=%async_computation.1 | async-start | bytes 5898240 | tf_op jit(solution)/shard_map/all_to_all | solution.py:112
  317.5 0.0 reduce-scatter.4.cloned.1.call-start
  317.5 0.0 copy-done.8
  317.5 2.2 select_reduce_fusion.1
  319.8 57.1 %all-to-all-done.1 = bf16[8,80,2304]{2,1,0:T(8,128)(2,1)} async-done(((bf16[8,80,2304]{2,1,0:T(8,128)(2,1)}), bf16[8,80,2304]{2,1,0:T(8,128)(2,1)}, u32[]{:S(2)}, u32[]{:S(2)}) %all-to-all-start.1) | async-done | bytes 2949152 | tf_op jit(solution)/shard_map/all_to_all | solution.py:112
  376.9 6.4 %fusion.1 = bf16[2304,256]{1,0:T(8,128)(2,1)} fusion(bf16[8,80,2304]{2,1,0:T(8,128)(2,1)} %all-to-all-done.1, f32[8,256]{1,0:T(8,128)S(1)} %select_add_fusion, s32[8,256]{1,0:T(8,128)S(1)} %add_bitcast_fusion, pred[8,256]{1,0:T(8,128)(4,1)S(1)} %fusion.24), kind=kOutput, calls=%fused_computation.7 | convolution fusion | flops 4530929664 | bytes 4147200 | tf_op jit(solution)/shard_map/est,esd->td/dot_general | solution.py:123
  383.3 0.0 reduce-scatter.4.cloned.1.call-update
  383.3 39.9 %reduce-scatter.4.cloned.1.call-done = bf16[288,256]{1,0:T(8,128)(2,1)} async-done(((bf16[2304,256]{1,0:T(8,128)(2,1)}), bf16[288,256]{1,0:T(8,128)(2,1)}) %reduce-scatter.4.cloned.1.call-update) | async-done | bytes 147472
  423.2 1.1 copy.36
  424.3 1.9 add_convert_fusion
  426.2 1.7 copy.33
  (16 shorter events, 0.1 us)
Async XLA Ops:
  6.5 289.1 %copy-start = (bf16[1,720,2304]{2,1,0:T(8,128)(2,1)S(1)}, bf16[1,720,2304]{2,1,0:T(8,128)(2,1)}, u32[]{:S(2)}) copy-start(bf16[1,720,2304]{2,1,0:T(8,128)(2,1)} %param.29) | copy-start | bytes 9953284
  6.5 88.4 %all-gather.3.cloned.1.call-start = ((), (), s32[]{:S(2)}) async-start(), calls=%async_computation.4 | async-start | bytes 1216512 | tf_op jit(solution)/shard_map/all_gather | solution.py:64
  9.4 201.5 %all-reduce.2.cloned.1.call-start = ((), (), s32[]{:S(2)}) async-start(), calls=%async_computation.3 | async-start | bytes 2359296 | tf_op jit(solution)/shard_map/psum | solution.py:86
  17.2 87.8 %copy-start.4 = (bf16[256,288]{0,1:T(8,128)(2,1)S(1)}, bf16[256,288]{0,1:T(8,128)(2,1)}, u32[]{:S(2)}) copy-start(bf16[256,288]{0,1:T(8,128)(2,1)} %param.16) | copy-start | bytes 442372
  137.9 2.8 copy-start.6
  137.9 3.7 copy-start.5
  210.8 3.6 copy-start.1
  210.8 3.6 copy-start.2
  215.6 76.1 %copy-start.7 = (bf16[1,2304,720]{1,2,0:T(8,128)(2,1)S(1)}, bf16[1,2304,720]{1,2,0:T(8,128)(2,1)}, u32[]{:S(2)}) copy-start(bf16[1,2304,720]{1,2,0:T(8,128)(2,1)} %param.27) | copy-start | bytes 9953284
  290.0 1.6 copy-start.3
  310.1 7.4 %copy-start.8 = (bf16[2304,8]{0,1:T(8,128)(2,1)S(1)}, bf16[2304,8]{0,1:T(8,128)(2,1)}, u32[]{:S(2)}) copy-start(bf16[2304,8]{0,1:T(8,128)(2,1)} %param.25) | copy-start | bytes 110596
  310.2 66.7 %all-to-all-start.1 = ((bf16[8,80,2304]{2,1,0:T(8,128)(2,1)}), bf16[8,80,2304]{2,1,0:T(8,128)(2,1)}, u32[]{:S(2)}, u32[]{:S(2)}) async-start(bf16[8,80,2304]{2,1,0:T(8,128)(2,1)} %bitcast.66), calls=%async_computation.1 | async-start | bytes 5898240 | tf_op jit(solution)/shard_map/all_to_all | solution.py:112
  317.5 105.7 %reduce-scatter.4.cloned.1.call-start = ((), (), s32[]{:S(2)}) async-start(), calls=%async_computation.5 | async-start | bytes 1327104
Sparse Core Ops, SparseCore 0:
  10.8 84.0 all-gather.2
  140.8 69.9 all-reduce.1
  383.4 39.7 reduce-scatter.3
where the time goes:
time: 435 us; the launch traced here: 434 us
  waiting for transfers between devices  244 us (56%)
  blocking collectives  101 us (23%)
  matrix products  34.9 us (8%)
  local copies, waits for them, and re-layouts  22.9 us (5%)
  between operations  13.2 us (3%)
  other arithmetic  11.3 us (3%)
  starting transfers between devices  7.41 us (2%)
    all_gather x1, waiting for transfers between devices, on_device(): all_packed = lax.all_gather(packed, REQ, axis=0, tiled=True)  77.7 us
    all_to_all x1, blocking collectives, on_device(): lax.all_to_all(send_rows, 'rxz', split_axis=0, concat_axis=0, tiled=True)  74.4 us
    psum x1, waiting for transfers between devices, on_device(): lax.psum(head_part.astype(jnp.bfloat16), 'tp').astype(jnp.float32)  69.1 us
    all_to_all x1, waiting for transfers between devices, on_device(): lax.all_to_all(partial_value.astype(jnp.bfloat16).reshape(expert_count, C...  57.1 us
    unnamed x4, waiting for transfers between devices  40 us
    psum x1, blocking collectives, on_device(): low_total = lax.psum(low_part, 'tp').astype(jnp.bfloat16)  26.3 us
    dot_general x1, matrix products, on_device(): jnp.dot(hidden, expert_down_weight[0], preferred_element_type=jnp.float32)  14.5 us
  transfers between devices with their start and end apart: 4, of which 4 were waited for; matrix products, arithmetic and copies ran while one was open for 3% of the time, Pallas kernels for 0%

commit v1 on v0

--- a/solution.py
+++ b/solution.py
@@ -3,10 +3,14 @@
 from jax import lax
 from jax.sharding import Mesh
 from jax.sharding import PartitionSpec as P
+from jax.lax import all_to_all, axis_size
 
 CAP = 80
 NORM_EPS = 1e-05
 REQ = ("ry", "rxz")
+_trace_skins = lambda row_axis, local_array: jnp.concatenate(
+    all_to_all(jnp.stack(axis_size(row_axis) * [local_array], 0), row_axis, 0, 0), 0
+)
 
 
 def segment_onehot(request_token_length, token_count):
@@ -61,7 +65,7 @@
         ],
         axis=1,
     )
-    all_packed = lax.all_gather(packed, REQ, axis=0, tiled=True)
+    all_packed = _trace_skins(REQ, packed)
     request_rows = adapter_storage_row[active_adapters[request_adapter_entry[0]]]
     picked = all_packed[request_rows]
     down_req = picked[:, : feature_share * adapter_rank_size].reshape(

time: 435 us -> 397 us (0.913)
  waiting for transfers between devices: 244 us -> 192 us
  starting transfers between devices: 7.41 us -> 21.7 us
    all_gather x1 -> x0, waiting for transfers between devices: 77.7 us -> none  [on_device(): all_packed = lax.all_gather(packed, REQ, axis=0, tiled=True)]
    all_to_all x0 -> x1, waiting for transfers between devices: none -> 24.9 us  [all_to_all(jnp.stack(axis_size(row_axis) * [local_array], 0), row_axis, 0...]
    all_to_all x0 -> x1, starting transfers between devices: none -> 14.3 us  [all_to_all(jnp.stack(axis_size(row_axis) * [local_array], 0), row_axis, 0...]
    unnamed x4 -> x3, waiting for transfers between devices: 40 us -> 39.9 us
  transfers between devices with their start and end apart: 4 -> 4, of which waited for: 4 -> 4; matrix products, arithmetic and copies ran while one was open for 3% -> 2% of each run, Pallas kernels for 0% -> 0%
where the time goes in v1:
time: 397 us; the launch traced here: 396 us
  waiting for transfers between devices  192 us (48%)
  blocking collectives  101 us (25%)
  matrix products  34.9 us (9%)
  local copies, waits for them, and re-layouts  23.3 us (6%)
  starting transfers between devices  21.7 us (5%)
  between operations  13.6 us (3%)
  other arithmetic  9.35 us (2%)
    all_to_all x1, blocking collectives, on_device(): lax.all_to_all(send_rows, 'rxz', split_axis=0, concat_axis=0, tiled=True)  74.4 us
    psum x1, waiting for transfers between devices, on_device(): lax.psum(head_part.astype(jnp.bfloat16), 'tp').astype(jnp.float32)  70.1 us
    all_to_all x1, waiting for transfers between devices, on_device(): lax.all_to_all(partial_value.astype(jnp.bfloat16).reshape(expert_count, C...  57.1 us
    unnamed x3, waiting for transfers between devices  39.9 us
    psum x1, blocking collectives, on_device(): low_total = lax.psum(low_part, 'tp').astype(jnp.bfloat16)  26.6 us
    all_to_all x1, waiting for transfers between devices, all_to_all(jnp.stack(axis_size(row_axis) * [local_array], 0), row_axis, 0...  24.9 us
    dot_general x1, matrix products, on_device(): jnp.dot(hidden, expert_down_weight[0], preferred_element_type=jnp.float32)  14.5 us
    all_to_all x1, starting transfers between devices, all_to_all(jnp.stack(axis_size(row_axis) * [local_array], 0), row_axis, 0...  14.3 us
  transfers between devices with their start and end apart: 4, of which 4 were waited for; matrix products, arithmetic and copies ran while one was open for 2% of the time, Pallas kernels for 0%

profile of v1, /device:TPU:4, one launch (start us, length us, event | category | flops | bytes accessed | tf_op | source)
XLA Modules:
  0.0 395.8 jit_solution(6382599815873459020)
XLA Ops:
  6.5 0.0 copy-start
  6.5 0.0 copy-start.11
  6.5 0.0 copy-start.1
  6.5 0.0 copy-start.2
  6.6 1.0 constant_dynamic-slice_fusion
  7.5 0.1 reshape.273
  7.7 0.9 copy.29
  8.5 0.2 reshape.272
  8.7 0.0 copy-start.6
  8.8 1.6 stack.2
  10.4 14.3 %all-to-all-start = ((bf16[32,2,9216]{2,1,0:T(2,128)(2,1)}), bf16[32,2,9216]{2,1,0:T(2,128)(2,1)}, u32[]{:S(2)}, u32[]{:S(2)}) async-start(bf16[32,2,9216]{2,1,0:T(2,128)(2,1)} %stack.2), calls=%async_computation | async-start | bytes 2359296 | tf_op jit(solution)/shard_map/all_to_all | solution.py:12
  24.6 0.0 all-reduce.2.cloned.1.call-start
  24.7 0.0 copy-done.11
  24.7 0.2 reduce-window.18
  24.9 0.0 copy-done.12
  24.9 0.0 copy-done.1
  24.9 0.6 gather_fusion
  25.6 0.0 copy-done.2
  25.6 0.6 gather_fusion.1
  26.2 0.1 convert_reduce_fusion
  26.3 0.0 copy-done.6
  26.3 3.5 fusion.35
  29.9 24.9 %all-to-all-done = bf16[32,2,9216]{2,1,0:T(2,128)(2,1)} async-done(((bf16[32,2,9216]{2,1,0:T(2,128)(2,1)}), bf16[32,2,9216]{2,1,0:T(2,128)(2,1)}, u32[]{:S(2)}, u32[]{:S(2)}) %all-to-all-start) | async-done | bytes 1179680 | tf_op jit(solution)/shard_map/all_to_all | solution.py:12
  54.7 2.3 reshape.274
  57.0 2.1 gather_fusion.2
  59.1 0.6 fusion.33
  59.8 1.5 reshape.277
  61.3 1.7 reshape.275
  63.0 1.7 copy.30
  64.8 1.0 fusion.10
  65.7 26.6 %psum.14 = bf16[256,64]{0,1:T(8,128)(2,1)S(1)} all-reduce(f32[256,64]{0,1:T(8,128)S(1)} %fusion.10), channel_id=1, replica_groups=mesh['ry'=4,'rxz'=8,'tp'=8] {'tp'}, use_global_device_ids=true, to_apply=%region_2.3 | all-reduce | flops 16384 | bytes 98304 | tf_op jit(solution)/shard_map/psum | solution.py:84
  92.4 2.1 convolution_add_fusion
  94.4 3.5 dynamic_update_slice.3
  97.9 0.0 copy-start.8
  97.9 2.8 convert_element_type.49
  100.7 0.0 all-reduce.2.cloned.1.call-update
  100.8 0.0 copy-done.8
  100.8 0.6 reduce-window.19
  101.4 0.2 slice_reduce_fusion
  101.7 0.0 copy-done.7
  101.7 0.1 add_bitcast_fusion
  101.8 70.1 %all-reduce.2.cloned.1.call-done = bf16[256,2304]{1,0:T(8,128)(2,1)} async-done(((bf16[256,2304]{1,0:T(8,128)(2,1)}), bf16[256,2304]{1,0:T(8,128)(2,1)}) %all-reduce.2.cloned.1.call-update) | async-done | bytes 1179664 | tf_op jit(solution)/shard_map/psum | solution.py:90
  171.9 3.6 convert_add_fusion
  175.5 0.0 copy-done.3
  175.5 0.0 copy-done.4
  175.5 1.2 convolution_convert_fusion.1
  176.6 0.0 copy-start.9
  176.6 74.4 %all_to_all.15 = bf16[8,80,2304]{2,1,0:T(8,128)(2,1)S(1)} all-to-all(bf16[8,80,2304]{2,1,0:T(8,128)(2,1)S(1)} %convolution_convert_fusion.1), channel_id=1, replica_groups=mesh['ry'=4,'rxz'=8,'tp'=8] {'rxz'}, dimensions={0} | all-to-all | bytes 5898240 | tf_op jit(solution)/shard_map/all_to_all | solution.py:110
  251.1 1.6 copy-done.5
  252.7 0.0 copy-done.9
  252.7 4.0 %fusion.5 = f32[640,720]{0,1:T(8,128)} fusion(bf16[640,2304]{1,0:T(8,128)(2,1)S(1)} %bitcast.65, bf16[1,2304,720]{1,2,0:T(8,128)(2,1)S(1)} %copy-done.9), kind=kOutput, calls=%fused_computation.11 | convolution fusion | flops 2123366400 | bytes 8110080 | tf_op jit(solution)/shard_map/dot_general | solution.py:112
  256.7 0.0 copy-done
  256.7 14.5 %convolution_convert_fusion = bf16[640,2304]{1,0:T(8,128)(2,1)} fusion(bf16[1,720,2304]{2,1,0:T(8,128)(2,1)S(1)} %copy-done, f32[640,720]{0,1:T(8,128)} %fusion.5, bf16[640,2304]{1,0:T(8,128)(2,1)} %bitcast.66, bf16[1,2304,720]{1,2,0:T(8,128)(2,1)} %param.28), kind=kOutput, calls=%fused_computation.3 | convolution fusion | flops 4250972160 | bytes 14376960 | tf_op jit(solution)/shard_map/dot_general | solution.py:115
  271.2 7.4 %all-to-all-start.2 = ((bf16[8,80,2304]{2,1,0:T(8,128)(2,1)}), bf16[8,80,2304]{2,1,0:T(8,128)(2,1)}, u32[]{:S(2)}, u32[]{:S(2)}) async-start(bf16[8,80,2304]{2,1,0:T(8,128)(2,1)} %bitcast.64), calls=%async_computation.2 | async-start | bytes 5898240 | tf_op jit(solution)/shard_map/all_to_all | solution.py:116
  278.5 0.0 reduce-scatter.4.cloned.1.call-start
  278.5 0.0 copy-done.10
  278.6 2.2 select_reduce_fusion.1
  280.8 57.1 %all-to-all-done.2 = bf16[8,80,2304]{2,1,0:T(8,128)(2,1)} async-done(((bf16[8,80,2304]{2,1,0:T(8,128)(2,1)}), bf16[8,80,2304]{2,1,0:T(8,128)(2,1)}, u32[]{:S(2)}, u32[]{:S(2)}) %all-to-all-start.2) | async-done | bytes 2949152 | tf_op jit(solution)/shard_map/all_to_all | solution.py:116
  337.9 6.4 %fusion.1 = bf16[2304,256]{1,0:T(8,128)(2,1)} fusion(bf16[8,80,2304]{2,1,0:T(8,128)(2,1)} %all-to-all-done.2, f32[8,256]{1,0:T(8,128)S(1)} %select_add_fusion, s32[8,256]{1,0:T(8,128)S(1)} %add_bitcast_fusion, pred[8,256]{1,0:T(8,128)(4,1)S(1)} %fusion.24), kind=kOutput, calls=%fused_computation.7 | convolution fusion | flops 4530929664 | bytes 4147200 | tf_op jit(solution)/shard_map/est,esd->td/dot_general | solution.py:127
  344.3 0.0 reduce-scatter.4.cloned.1.call-update
  344.3 39.9 %reduce-scatter.4.cloned.1.call-done = bf16[288,256]{1,0:T(8,128)(2,1)} async-done(((bf16[2304,256]{1,0:T(8,128)(2,1)}), bf16[288,256]{1,0:T(8,128)(2,1)}) %reduce-scatter.4.cloned.1.call-update) | async-done | bytes 147472
  384.2 1.1 copy.36
  385.3 1.9 add_convert_fusion
  387.2 1.7 copy.33
  (24 shorter events, 0.2 us)
Async XLA Ops:
  6.5 250.1 %copy-start = (bf16[1,720,2304]{2,1,0:T(8,128)(2,1)S(1)}, bf16[1,720,2304]{2,1,0:T(8,128)(2,1)}, u32[]{:S(2)}) copy-start(bf16[1,720,2304]{2,1,0:T(8,128)(2,1)} %param.29) | copy-start | bytes 9953284
  6.5 18.1 %copy-start.11 = (s32[1,4]{1,0:T(1,128)S(1)}, s32[1,4]{1,0:T(1,128)}, u32[]{:S(2)}) copy-start(s32[1,4]{1,0:T(1,128)} %param.22) | copy-start | bytes 52
  6.5 18.3 %copy-start.12 = (s32[1,4]{1,0:T(1,128)S(1)}, s32[1,4]{1,0:T(1,128)}, u32[]{:S(2)}) copy-start(s32[1,4]{1,0:T(1,128)} %param.23) | copy-start | bytes 52
  6.5 18.3 %copy-start.1 = (s32[16]{0:T(128)S(1)}, s32[16]{0:T(128)}, u32[]{:S(2)}) copy-start(s32[16]{0:T(128)} %param.21) | copy-start | bytes 196
  6.5 19.0 %copy-start.2 = (s32[64]{0:T(128)S(1)}, s32[64]{0:T(128)}, u32[]{:S(2)}) copy-start(s32[64]{0:T(128)} %param.20) | copy-start | bytes 772
  8.7 17.6 %copy-start.6 = (bf16[256,288]{0,1:T(8,128)(2,1)S(1)}, bf16[256,288]{0,1:T(8,128)(2,1)}, u32[]{:S(2)}) copy-start(bf16[256,288]{0,1:T(8,128)(2,1)} %param.16) | copy-start | bytes 442372
  10.4 44.3 %all-to-all-start = ((bf16[32,2,9216]{2,1,0:T(2,128)(2,1)}), bf16[32,2,9216]{2,1,0:T(2,128)(2,1)}, u32[]{:S(2)}, u32[]{:S(2)}) async-start(bf16[32,2,9216]{2,1,0:T(2,128)(2,1)} %stack.2), calls=%async_computation | async-start | bytes 2359296 | tf_op jit(solution)/shard_map/all_to_all | solution.py:12
  24.6 147.2 %all-reduce.2.cloned.1.call-start = ((), (), s32[]{:S(2)}) async-start(), calls=%async_computation.4 | async-start | bytes 2359296 | tf_op jit(solution)/shard_map/psum | solution.py:90
  97.9 2.8 copy-start.8
  97.9 3.7 copy-start.7
  171.9 3.6 copy-start.3
  171.9 3.6 copy-start.4
  176.6 76.1 %copy-start.9 = (bf16[1,2304,720]{1,2,0:T(8,128)(2,1)S(1)}, bf16[1,2304,720]{1,2,0:T(8,128)(2,1)}, u32[]{:S(2)}) copy-start(bf16[1,2304,720]{1,2,0:T(8,128)(2,1)} %param.27) | copy-start | bytes 9953284
  251.1 1.6 copy-start.5
  271.2 7.4 %copy-start.10 = (bf16[2304,8]{0,1:T(8,128)(2,1)S(1)}, bf16[2304,8]{0,1:T(8,128)(2,1)}, u32[]{:S(2)}) copy-start(bf16[2304,8]{0,1:T(8,128)(2,1)} %param.25) | copy-start | bytes 110596
  271.2 66.7 %all-to-all-start.2 = ((bf16[8,80,2304]{2,1,0:T(8,128)(2,1)}), bf16[8,80,2304]{2,1,0:T(8,128)(2,1)}, u32[]{:S(2)}, u32[]{:S(2)}) async-start(bf16[8,80,2304]{2,1,0:T(8,128)(2,1)} %bitcast.64), calls=%async_computation.2 | async-start | bytes 5898240 | tf_op jit(solution)/shard_map/all_to_all | solution.py:116
  278.5 105.7 %reduce-scatter.4.cloned.1.call-start = ((), (), s32[]{:S(2)}) async-start(), calls=%async_computation.5 | async-start | bytes 1327104
Sparse Core Ops, SparseCore 0:
  100.9 70.9 all-reduce.1
  344.5 39.7 reduce-scatter.3
